TPU v7x, 512 devices: a whole 4x4x16 slice. The times are simulated.
512 devices in a mesh: dir: 8 (over x, core), texel: 64 (over z, y).
Axes of the slice: x: 4, y: 4, z: 16, core: 2. Of those that a mesh axis runs over, the one named last changes fastest.
Arguments:
- texels: bfloat16 [4096, 50176], P('texel', 'dir'), may hold values from -6 to 6
- labels: int32 [4096, 1], P('texel'), may hold values from 0 to 127; in each aligned block of 64 rows (0 to 63, 64 to 127, ...) at most 2 rows name the same one
- start_basis: bfloat16 [64, 50176], P(None, 'dir'), may hold values from -0.02734375 to 0.02734375
Outputs:
- coefficients: float32 [4096, 64], P('texel')
- bases: bfloat16 [128, 64, 50176], P('texel', None, 'dir')
Inputs may be any that keep to these rules, and one draw needn't show every extreme that they name: `labels`: among the rows of one index of texel (an aligned block of 64 rows) no cluster is named by more than 2 rows, a bound that some block reaches in every draw.
All inputs are finite; a program needn't handle non-finite values.
Results may differ from a plain program's by a relative error of at most 0.012.
Values may be sent and summed in bfloat16 or wider, within the bound.
A program may use at most 64 MiB of HBM per device.

v0:
```python
import jax
import jax.numpy as jnp
from jax import lax
from jax.sharding import PartitionSpec as P

COLS = 50176
K = 64
CL_DEV = 2
ITERS = 2
ridge_share = 0.05


def per_device(texels, labels, start_basis):
    row_count = texels.shape[0]
    col_width = texels.shape[1]
    groups = lax.axis_size("texel")
    slot_cap = max(2, 2 * row_count // (CL_DEV * groups))
    label_col = labels[:, 0]
    owners = label_col // CL_DEV
    local_idx = label_col % CL_DEV
    row_ids = jnp.arange(row_count, dtype=jnp.int32)
    matches = (label_col[None, :] == label_col[:, None]) & (row_ids[None, :] < row_ids[:, None])
    slot_rank = jnp.sum(matches.astype(jnp.int32), axis=1)
    slot_of_row = local_idx * (groups * slot_cap) + owners * slot_cap + slot_rank
    total_slots = CL_DEV * groups * slot_cap
    slot_ids = jnp.arange(total_slots, dtype=jnp.int32)
    slot_hit = slot_of_row[None, :] == slot_ids[:, None]
    source_row = jnp.sum(jnp.where(slot_hit, row_ids[None, :], 0), axis=1)
    filled = jnp.any(slot_hit, axis=1)
    outgoing = jnp.where(
        filled[:, None], jnp.take(texels, source_row, axis=0), jnp.zeros((), texels.dtype)
    )
    outgoing = outgoing.reshape(CL_DEV, groups * slot_cap, col_width)
    received = lax.all_to_all(outgoing, "texel", split_axis=1, concat_axis=1, tiled=True)
    ridge_term = jnp.float32(ridge_share * COLS)
    identity = jnp.broadcast_to(jnp.eye(K, dtype=jnp.float32), (CL_DEV, K, K))
    basis_now = jnp.broadcast_to(start_basis, (CL_DEV, K, col_width))
    highest = lax.Precision.HIGHEST
    for sweep in range(ITERS):
        local_proj = jnp.einsum(
            "crw,ckw->crk", received, basis_now, preferred_element_type=jnp.float32
        )
        summed_proj = lax.psum(local_proj, "dir")
        projected = summed_proj.astype(jnp.bfloat16)
        widened = jnp.einsum(
            "crk,crw->ckw", projected, received, preferred_element_type=jnp.float32
        ) + ridge_term * basis_now.astype(jnp.float32)
        gram_mat = lax.psum(
            jnp.einsum(
                "ckw,clw->ckl",
                widened,
                widened,
                precision=highest,
                preferred_element_type=jnp.float32,
            ),
            "dir",
        )
        lower_tri = jnp.linalg.cholesky(gram_mat)
        inverse = jax.scipy.linalg.solve_triangular(lower_tri, identity, lower=True)
        basis_now = jnp.einsum(
            "ckl,clw->ckw", inverse, widened, precision=highest, preferred_element_type=jnp.float32
        ).astype(jnp.bfloat16)
    partial_value = jnp.einsum(
        "crw,ckw->crk", received, basis_now, preferred_element_type=jnp.float32
    )
    summed = lax.psum(partial_value.astype(jnp.bfloat16), "dir").astype(jnp.float32)
    returned = lax.all_to_all(
        summed.astype(jnp.bfloat16), "texel", split_axis=1, concat_axis=1, tiled=True
    ).astype(summed.dtype)
    coefficients = returned.reshape(total_slots, K)[slot_of_row]
    return (coefficients, basis_now)


def solution(mesh):
    in_specs = (P("texel", "dir"), P("texel", None), P(None, "dir"))
    out_specs = (P("texel", None), P("texel", None, "dir"))
    return jax.shard_map(
        per_device, mesh=mesh, in_specs=in_specs, out_specs=out_specs, check_vma=False
    )
```

profile of v0, /device:TPU:8, one launch (start us, length us, event | category | flops | bytes accessed | tf_op | source)
XLA Modules:
  0.0 404.1 jit_solution(9749141329993377410)
XLA Ops:
  0.6 0.0 copy-start
  0.6 0.9 convert_reduce_fusion
  1.6 0.7 fusion.27
  2.2 0.1 select_reduce_fusion.2
  2.3 0.1 fusion.18
  2.5 0.1 copy.65
  2.6 0.1 copy.64
  2.8 0.0 copy-done
  2.8 4.2 %gather_fusion = bf16[256,6272]{1,0:T(8,128)(2,1)} fusion(bf16[64,6272]{1,0:T(8,128)(2,1)S(1)} %copy-done, s32[1024]{0:T(1024)S(1)} %pad_clamp_fusion.1), kind=kCustom, calls=%fused_computation | custom fusion | bytes 6423552 | tf_op jit(solution)/shard_map/jit(_take)/gather | solution.py:31
  7.0 8.2 %broadcast_select_fusion.1 = bf16[2,128,6272]{2,0,1:T(2,128)(2,1)} fusion(pred[2,128]{0,1:T(8,128)(4,1)S(1)} %copy.64, pred[2,128]{0,1:T(8,128)(4,1)S(1)} %copy.65, bf16[2,128,6272]{2,1,0:T(8,128)(2,1)} %bitcast.47), kind=kLoop, calls=%fused_computation.7 | loop fusion | flops 3211264 | bytes 6423040 | tf_op jit(solution)/shard_map/jit(_where)/select_n | solution.py:30
  15.2 0.0 copy-start.4
  15.2 19.0 %all-to-all-start = ((bf16[2,128,6272]{2,0,1:T(2,128)(2,1)}), bf16[2,128,6272]{2,0,1:T(2,128)(2,1)}, u32[]{:S(2)}, u32[]{:S(2)}) async-start(bf16[2,128,6272]{2,0,1:T(2,128)(2,1)} %broadcast_select_fusion.1), calls=%async_computation | async-start | bytes 6422528 | tf_op jit(solution)/shard_map/all_to_all | solution.py:34
  34.2 0.0 copy-done.4
  34.2 0.1 convert_multiply_fusion
  34.4 147.6 %all-to-all-done = bf16[2,128,6272]{2,0,1:T(2,128)(2,1)} async-done(((bf16[2,128,6272]{2,0,1:T(2,128)(2,1)}), bf16[2,128,6272]{2,0,1:T(2,128)(2,1)}, u32[]{:S(2)}, u32[]{:S(2)}) %all-to-all-start) | async-done | bytes 3211296 | tf_op jit(solution)/shard_map/all_to_all | solution.py:34
  182.0 3.1 fusion.2
  185.1 24.1 %psum.35 = bf16[2,128,64]{1,2,0:T(8,128)(2,1)S(1)} all-reduce(f32[2,128,64]{1,2,0:T(8,128)S(1)} %fusion.2), channel_id=1, replica_groups=mesh['dir'=8,'texel'=64] {'dir'}, use_global_device_ids=true, to_apply=%region_3.4 | all-reduce | flops 16384 | bytes 98304 | tf_op jit(solution)/shard_map/psum | solution.py:43
  209.3 2.7 convolution_add_fusion.1
  212.0 0.0 copy-start.2
  212.0 1.7 copy-done.2
  213.7 3.1 fusion.32
  216.8 23.9 %psum.36 = f32[2,64,64]{1,2,0:T(8,128)S(1)} all-reduce(f32[2,64,64]{1,2,0:T(8,128)S(1)} %fusion.32), channel_id=1, replica_groups=mesh['dir'=8,'texel'=64] {'dir'}, use_global_device_ids=true, to_apply=%region_4.5 | all-reduce | flops 8192 | bytes 65536 | tf_op jit(solution)/shard_map/psum | solution.py:48
  240.8 0.1 copy.70
  240.9 11.7 %custom-call.8 = f32[2,64,64]{2,1,0:T(8,128)S(1)} custom-call(f32[2,64,64]{2,1,0:T(8,128)S(1)} %fusion.17), custom_call_target="Cholesky" | custom-call | tf_op jit(solution)/shard_map/jit(cholesky)/cholesky | solution.py:58
  252.7 0.1 compare_reduce_fusion.1
  252.8 0.1 select_bitcast_fusion.1
  252.9 9.8 %custom-call.9 = f32[2,1,64,64]{2,3,1,0:T(8,128)S(1)} custom-call(f32[2,1,64,64]{3,2,1,0:T(8,128)S(1)} %select_bitcast_fusion.1), custom_call_target="InvertDiagBlocksLowerTriangular" | custom-call | tf_op jit(solution)/shard_map/jit(_solve_triangular)/vmap()/triangular_solve | solution.py:59
  262.7 0.3 fusion.15
  263.0 4.7 %convolution_convert_fusion.1 = bf16[2,64,6272]{2,1,0:T(8,128)(2,1)S(1)} fusion(f32[2,64,64]{2,1,0:T(8,128)S(1)} %fusion.15, f32[2,64,6272]{2,1,0:T(8,128)} %copy-done.2), kind=kOutput, calls=%fused_computation.5 | convolution fusion | flops 617365504 | bytes 4849664 | tf_op jit(solution)/shard_map/ckl,clw->ckw/dot_general | solution.py:60
  267.7 3.1 fusion.4
  270.9 24.2 %psum.37 = bf16[2,128,64]{1,2,0:T(8,128)(2,1)S(1)} all-reduce(f32[2,128,64]{1,2,0:T(8,128)S(1)} %fusion.4), channel_id=1, replica_groups=mesh['dir'=8,'texel'=64] {'dir'}, use_global_device_ids=true, to_apply=%region_7.10 | all-reduce | flops 16384 | bytes 98304 | tf_op jit(solution)/shard_map/psum | solution.py:43
  295.1 2.6 convolution_add_fusion
  297.7 0.0 copy-start.1
  297.7 1.7 copy-done.1
  299.4 3.1 fusion.33
  302.5 23.9 %psum.38 = f32[2,64,64]{1,2,0:T(8,128)S(1)} all-reduce(f32[2,64,64]{1,2,0:T(8,128)S(1)} %fusion.33), channel_id=1, replica_groups=mesh['dir'=8,'texel'=64] {'dir'}, use_global_device_ids=true, to_apply=%region_8.11 | all-reduce | flops 8192 | bytes 65536 | tf_op jit(solution)/shard_map/psum | solution.py:48
  326.5 0.1 copy.75
  326.6 11.7 %custom-call.10 = f32[2,64,64]{2,1,0:T(8,128)S(1)} custom-call(f32[2,64,64]{2,1,0:T(8,128)S(1)} %fusion.14), custom_call_target="Cholesky" | custom-call | tf_op jit(solution)/shard_map/jit(cholesky)/cholesky | solution.py:58
  338.4 0.1 compare_reduce_fusion
  338.5 0.1 select_bitcast_fusion
  338.6 9.8 %custom-call.11 = f32[2,1,64,64]{2,3,1,0:T(8,128)S(1)} custom-call(f32[2,1,64,64]{3,2,1,0:T(8,128)S(1)} %select_bitcast_fusion), custom_call_target="InvertDiagBlocksLowerTriangular" | custom-call | tf_op jit(solution)/shard_map/jit(_solve_triangular)/vmap()/triangular_solve | solution.py:59
  348.4 0.3 fusion.12
  348.7 4.7 %convolution_convert_fusion = bf16[2,64,6272]{2,1,0:T(8,128)(2,1)S(1)} fusion(f32[2,64,64]{2,1,0:T(8,128)S(1)} %fusion.12, f32[2,64,6272]{2,1,0:T(8,128)} %copy-done.1), kind=kOutput, calls=%fused_computation.4 | convolution fusion | flops 617365504 | bytes 4849664 | tf_op jit(solution)/shard_map/ckl,clw->ckw/dot_general | solution.py:60
  353.4 0.0 copy-start.3
  353.5 0.0 copy-start.5
  353.5 3.7 fusion.8
  357.2 23.6 %psum.39 = bf16[2,128,64]{1,2,0:T(8,128)(2,1)S(1)} all-reduce(bf16[2,128,64]{1,2,0:T(8,128)(2,1)S(1)} %fusion.8), channel_id=1, replica_groups=mesh['dir'=8,'texel'=64] {'dir'}, use_global_device_ids=true, to_apply=%region_9.12 | all-reduce | flops 16384 | bytes 65536 | tf_op jit(solution)/shard_map/psum | solution.py:66
  380.8 0.1 copy.78
  381.0 0.7 reshape.126
  381.7 7.3 %all-to-all-start.1 = ((bf16[64,2,128]{2,1,0:T(2,128)(2,1)}), bf16[64,2,128]{2,1,0:T(2,128)(2,1)S(1)}, u32[]{:S(2)}, u32[]{:S(2)}) async-start(bf16[64,2,128]{2,1,0:T(2,128)(2,1)} %reshape.126), calls=%async_computation.1 | async-start | bytes 65536 | tf_op jit(solution)/shard_map/all_to_all | solution.py:67
  389.0 0.0 copy-done.5
  389.0 13.6 %all-to-all-done.1 = bf16[64,2,128]{2,1,0:T(2,128)(2,1)S(1)} async-done(((bf16[64,2,128]{2,1,0:T(2,128)(2,1)}), bf16[64,2,128]{2,1,0:T(2,128)(2,1)S(1)}, u32[]{:S(2)}, u32[]{:S(2)}) %all-to-all-start.1) | async-done | bytes 32800 | tf_op jit(solution)/shard_map/all_to_all | solution.py:67
  402.6 0.1 reshape.127
  402.7 0.1 copy.79
  402.8 0.1 copy.86
  402.9 1.2 gather_fusion.1
  404.1 0.0 copy-done.3
  (12 shorter events, 0.1 us)
Async XLA Ops:
  0.6 2.1 copy-start
  15.2 19.1 %copy-start.4 = (bf16[64,6272]{1,0:T(8,128)(2,1)S(1)}, bf16[64,6272]{1,0:T(8,128)(2,1)}, u32[]{:S(2)}) copy-start(bf16[64,6272]{1,0:T(8,128)(2,1)} %param.8) | copy-start | bytes 2408452
  15.2 166.8 %all-to-all-start = ((bf16[2,128,6272]{2,0,1:T(2,128)(2,1)}), bf16[2,128,6272]{2,0,1:T(2,128)(2,1)}, u32[]{:S(2)}, u32[]{:S(2)}) async-start(bf16[2,128,6272]{2,0,1:T(2,128)(2,1)} %broadcast_select_fusion.1), calls=%async_computation | async-start | bytes 6422528 | tf_op jit(solution)/shard_map/all_to_all | solution.py:34
  212.0 1.7 copy-start.2
  297.7 1.7 copy-start.1
  353.4 50.7 %copy-start.3 = (bf16[2,64,6272]{2,1,0:T(8,128)(2,1)}, bf16[2,64,6272]{2,1,0:T(8,128)(2,1)S(1)}, u32[]{:S(2)}) copy-start(bf16[2,64,6272]{2,1,0:T(8,128)(2,1)S(1)} %convolution_convert_fusion) | copy-start | bytes 4816900
  353.5 35.5 %copy-start.5 = (s32[64,1]{0,1:T(1,128)S(1)}, s32[64,1]{0,1:T(1,128)}, u32[]{:S(2)}) copy-start(s32[64,1]{0,1:T(1,128)} %param.7) | copy-start | bytes 772
  381.7 21.0 %all-to-all-start.1 = ((bf16[64,2,128]{2,1,0:T(2,128)(2,1)}), bf16[64,2,128]{2,1,0:T(2,128)(2,1)S(1)}, u32[]{:S(2)}, u32[]{:S(2)}) async-start(bf16[64,2,128]{2,1,0:T(2,128)(2,1)} %reshape.126), calls=%async_computation.1 | async-start | bytes 65536 | tf_op jit(solution)/shard_map/all_to_all | solution.py:67
where the time goes:
time: 405 us; the launch traced here: 404 us
  waiting for transfers between devices  161 us (40%)
  blocking collectives  120 us (30%)
  other arithmetic  53.8 us (13%)
  matrix products  31.7 us (8%)
  starting transfers between devices  26.3 us (6%)
  local copies, waits for them, and re-layouts  10.4 us (3%)
    all_to_all x1, waiting for transfers between devices, per_device(): lax.all_to_all(outgoing, 'texel', split_axis=1, concat_axis=1, tiled=True)  148 us
    psum x2, blocking collectives, per_device(): summed_proj = lax.psum(local_proj, 'dir')  48.3 us
    psum x2, blocking collectives, per_device(): lax.psum(jnp.einsum('ckw,clw->ckl', widened, widened, precision=highest,...  47.9 us
    another operation x7, other arithmetic, per_device(): lower_tri = jnp.linalg.cholesky(gram_mat)  23.8 us
    psum x1, blocking collectives, per_device(): lax.psum(partial_value.astype(jnp.bfloat16), 'dir').astype(jnp.float32)  23.6 us
    another operation x5, other arithmetic, per_device(): inverse = jax.scipy.linalg.solve_triangular(lower_tri, identity, lower=True)  19.8 us
    all_to_all x1, starting transfers between devices, per_device(): lax.all_to_all(outgoing, 'texel', split_axis=1, concat_axis=1, tiled=True)  19 us
    all_to_all x1, waiting for transfers between devices, per_device(): lax.all_to_all(summed.astype(jnp.bfloat16), 'texel', split_axis=1, concat...  13.6 us
  transfers between devices with their start and end apart: 2, of which 2 were waited for; matrix products, arithmetic and copies ran while one was open for 0% of the time, Pallas kernels for 0%

commit v1 on v0

--- a/solution.py
+++ b/solution.py
@@ -40,7 +40,7 @@
         local_proj = jnp.einsum(
             "crw,ckw->crk", received, basis_now, preferred_element_type=jnp.float32
         )
-        summed_proj = lax.psum(local_proj, "dir")
+        summed_proj = jnp.sum(lax.all_gather(local_proj, "dir"), axis=0)
         projected = summed_proj.astype(jnp.bfloat16)
         widened = jnp.einsum(
             "crk,crw->ckw", projected, received, preferred_element_type=jnp.float32

time: 405 us -> 385 us (0.951)
  blocking collectives: 120 us -> 101 us
    psum x2 -> x0, blocking collectives: 48.3 us -> none  [per_device(): summed_proj = lax.psum(local_proj, 'dir')]
    all_gather x0 -> x2, blocking collectives: none -> 27 us  [per_device(): summed_proj = jnp.sum(lax.all_gather(local_proj, 'dir'), axis=0)]
where the time goes in v1:
time: 385 us; the launch traced here: 384 us
  waiting for transfers between devices  161 us (42%)
  blocking collectives  101 us (26%)
  other arithmetic  53.8 us (14%)
  matrix products  31.7 us (8%)
  starting transfers between devices  25 us (6%)
  local copies, waits for them, and re-layouts  10.4 us (3%)
    all_to_all x1, waiting for transfers between devices, per_device(): lax.all_to_all(outgoing, 'texel', split_axis=1, concat_axis=1, tiled=True)  148 us
    psum x2, blocking collectives, per_device(): lax.psum(jnp.einsum('ckw,clw->ckl', widened, widened, precision=highest,...  50.4 us
    all_gather x2, blocking collectives, per_device(): summed_proj = jnp.sum(lax.all_gather(local_proj, 'dir'), axis=0)  27 us
    another operation x7, other arithmetic, per_device(): lower_tri = jnp.linalg.cholesky(gram_mat)  23.8 us
    psum x1, blocking collectives, per_device(): lax.psum(partial_value.astype(jnp.bfloat16), 'dir').astype(jnp.float32)  23.6 us
    another operation x5, other arithmetic, per_device(): inverse = jax.scipy.linalg.solve_triangular(lower_tri, identity, lower=True)  19.8 us
    all_to_all x1, starting transfers between devices, per_device(): lax.all_to_all(outgoing, 'texel', split_axis=1, concat_axis=1, tiled=True)  19 us
    all_to_all x1, waiting for transfers between devices, per_device(): lax.all_to_all(summed.astype(jnp.bfloat16), 'texel', split_axis=1, concat...  13.6 us
  transfers between devices with their start and end apart: 2, of which 2 were waited for; matrix products, arithmetic and copies ran while one was open for 0% of the time, Pallas kernels for 0%

profile of v1, /device:TPU:8, one launch (start us, length us, event | category | flops | bytes accessed | tf_op | source)
XLA Modules:
  0.0 384.1 jit_solution(2799998553661570240)
XLA Ops:
  0.6 0.0 copy-start
  0.6 0.9 convert_reduce_fusion
  1.6 0.7 fusion.27
  2.2 0.1 select_reduce_fusion.2
  2.3 0.1 fusion.18
  2.5 0.1 copy.65
  2.6 0.1 copy.64
  2.8 0.0 copy-done
  2.8 4.2 %gather_fusion = bf16[256,6272]{1,0:T(8,128)(2,1)} fusion(bf16[64,6272]{1,0:T(8,128)(2,1)S(1)} %copy-done, s32[1024]{0:T(1024)S(1)} %pad_clamp_fusion.1), kind=kCustom, calls=%fused_computation | custom fusion | bytes 6423552 | tf_op jit(solution)/shard_map/jit(_take)/gather | solution.py:31
  7.0 8.2 %broadcast_select_fusion.1 = bf16[2,128,6272]{2,0,1:T(2,128)(2,1)} fusion(pred[2,128]{0,1:T(8,128)(4,1)S(1)} %copy.64, pred[2,128]{0,1:T(8,128)(4,1)S(1)} %copy.65, bf16[2,128,6272]{2,1,0:T(8,128)(2,1)} %bitcast.49), kind=kLoop, calls=%fused_computation.7 | loop fusion | flops 3211264 | bytes 6423040 | tf_op jit(solution)/shard_map/jit(_where)/select_n | solution.py:30
  15.2 0.0 copy-start.4
  15.2 19.0 %all-to-all-start = ((bf16[2,128,6272]{2,0,1:T(2,128)(2,1)}), bf16[2,128,6272]{2,0,1:T(2,128)(2,1)}, u32[]{:S(2)}, u32[]{:S(2)}) async-start(bf16[2,128,6272]{2,0,1:T(2,128)(2,1)} %broadcast_select_fusion.1), calls=%async_computation | async-start | bytes 6422528 | tf_op jit(solution)/shard_map/all_to_all | solution.py:34
  34.2 0.0 copy-done.4
  34.2 0.1 convert_multiply_fusion
  34.4 147.6 %all-to-all-done = bf16[2,128,6272]{2,0,1:T(2,128)(2,1)} async-done(((bf16[2,128,6272]{2,0,1:T(2,128)(2,1)}), bf16[2,128,6272]{2,0,1:T(2,128)(2,1)}, u32[]{:S(2)}, u32[]{:S(2)}) %all-to-all-start) | async-done | bytes 3211296 | tf_op jit(solution)/shard_map/all_to_all | solution.py:34
  182.0 3.1 fusion.2
  185.1 13.6 %all-gather = f32[16,128,64]{1,2,0:T(8,128)S(1)} all-gather(f32[2,128,64]{1,2,0:T(8,128)S(1)} %fusion.2), channel_id=2, replica_groups=mesh['dir'=8,'texel'=64] {'dir'}, dimensions={0}, use_global_device_ids=true | all-gather | bytes 589824 | tf_op jit(solution)/shard_map/all_gather | solution.py:43
  198.8 2.7 convolution_add_fusion.1
  201.5 0.0 copy-start.2
  201.6 1.7 copy-done.2
  203.2 3.1 fusion.32
  206.4 26.2 %psum.21 = f32[2,64,64]{1,2,0:T(8,128)S(1)} all-reduce(f32[2,64,64]{1,2,0:T(8,128)S(1)} %fusion.32), channel_id=1, replica_groups=mesh['dir'=8,'texel'=64] {'dir'}, use_global_device_ids=true, to_apply=%region_4.5 | all-reduce | flops 8192 | bytes 65536 | tf_op jit(solution)/shard_map/psum | solution.py:48
  232.6 0.1 copy.70
  232.7 11.7 %custom-call.8 = f32[2,64,64]{2,1,0:T(8,128)S(1)} custom-call(f32[2,64,64]{2,1,0:T(8,128)S(1)} %fusion.17), custom_call_target="Cholesky" | custom-call | tf_op jit(solution)/shard_map/jit(cholesky)/cholesky | solution.py:58
  244.5 0.1 compare_reduce_fusion.1
  244.6 0.1 select_bitcast_fusion.1
  244.7 9.8 %custom-call.9 = f32[2,1,64,64]{2,3,1,0:T(8,128)S(1)} custom-call(f32[2,1,64,64]{3,2,1,0:T(8,128)S(1)} %select_bitcast_fusion.1), custom_call_target="InvertDiagBlocksLowerTriangular" | custom-call | tf_op jit(solution)/shard_map/jit(_solve_triangular)/vmap()/triangular_solve | solution.py:59
  254.5 0.3 fusion.15
  254.8 4.7 %convolution_convert_fusion.1 = bf16[2,64,6272]{2,1,0:T(8,128)(2,1)S(1)} fusion(f32[2,64,64]{2,1,0:T(8,128)S(1)} %fusion.15, f32[2,64,6272]{2,1,0:T(8,128)} %copy-done.2), kind=kOutput, calls=%fused_computation.5 | convolution fusion | flops 617365504 | bytes 4849664 | tf_op jit(solution)/shard_map/ckl,clw->ckw/dot_general | solution.py:60
  259.6 3.1 fusion.4
  262.7 13.3 %all-gather.1 = f32[16,128,64]{1,2,0:T(8,128)S(1)} all-gather(f32[2,128,64]{1,2,0:T(8,128)S(1)} %fusion.4), channel_id=3, replica_groups=mesh['dir'=8,'texel'=64] {'dir'}, dimensions={0}, use_global_device_ids=true | all-gather | bytes 589824 | tf_op jit(solution)/shard_map/all_gather | solution.py:43
  276.1 2.6 convolution_add_fusion
  278.7 0.0 copy-start.1
  278.7 1.7 copy-done.1
  280.4 3.1 fusion.33
  283.6 24.2 %psum.22 = f32[2,64,64]{1,2,0:T(8,128)S(1)} all-reduce(f32[2,64,64]{1,2,0:T(8,128)S(1)} %fusion.33), channel_id=1, replica_groups=mesh['dir'=8,'texel'=64] {'dir'}, use_global_device_ids=true, to_apply=%region_8.11 | all-reduce | flops 8192 | bytes 65536 | tf_op jit(solution)/shard_map/psum | solution.py:48
  307.8 0.1 copy.75
  307.9 11.7 %custom-call.10 = f32[2,64,64]{2,1,0:T(8,128)S(1)} custom-call(f32[2,64,64]{2,1,0:T(8,128)S(1)} %fusion.14), custom_call_target="Cholesky" | custom-call | tf_op jit(solution)/shard_map/jit(cholesky)/cholesky | solution.py:58
  319.6 0.1 compare_reduce_fusion
  319.8 0.1 select_bitcast_fusion
  319.8 9.8 %custom-call.11 = f32[2,1,64,64]{2,3,1,0:T(8,128)S(1)} custom-call(f32[2,1,64,64]{3,2,1,0:T(8,128)S(1)} %select_bitcast_fusion), custom_call_target="InvertDiagBlocksLowerTriangular" | custom-call | tf_op jit(solution)/shard_map/jit(_solve_triangular)/vmap()/triangular_solve | solution.py:59
  329.7 0.3 fusion.12
  330.0 4.7 %convolution_convert_fusion = bf16[2,64,6272]{2,1,0:T(8,128)(2,1)S(1)} fusion(f32[2,64,64]{2,1,0:T(8,128)S(1)} %fusion.12, f32[2,64,6272]{2,1,0:T(8,128)} %copy-done.1), kind=kOutput, calls=%fused_computation.4 | convolution fusion | flops 617365504 | bytes 4849664 | tf_op jit(solution)/shard_map/ckl,clw->ckw/dot_general | solution.py:60
  334.7 0.0 copy-start.3
  334.7 0.0 copy-start.5
  334.8 3.7 fusion.8
  338.5 23.6 %psum.23 = bf16[2,128,64]{1,2,0:T(8,128)(2,1)S(1)} all-reduce(bf16[2,128,64]{1,2,0:T(8,128)(2,1)S(1)} %fusion.8), channel_id=1, replica_groups=mesh['dir'=8,'texel'=64] {'dir'}, use_global_device_ids=true, to_apply=%region_9.12 | all-reduce | flops 16384 | bytes 65536 | tf_op jit(solution)/shard_map/psum | solution.py:66
  362.1 0.1 copy.78
  362.2 0.7 reshape.128
  363.0 6.0 %all-to-all-start.1 = ((bf16[64,2,128]{2,1,0:T(2,128)(2,1)}), bf16[64,2,128]{2,1,0:T(2,128)(2,1)S(1)}, u32[]{:S(2)}, u32[]{:S(2)}) async-start(bf16[64,2,128]{2,1,0:T(2,128)(2,1)} %reshape.128), calls=%async_computation.1 | async-start | bytes 65536 | tf_op jit(solution)/shard_map/all_to_all | solution.py:67
  368.9 0.0 copy-done.5
  369.0 13.6 %all-to-all-done.1 = bf16[64,2,128]{2,1,0:T(2,128)(2,1)S(1)} async-done(((bf16[64,2,128]{2,1,0:T(2,128)(2,1)}), bf16[64,2,128]{2,1,0:T(2,128)(2,1)S(1)}, u32[]{:S(2)}, u32[]{:S(2)}) %all-to-all-start.1) | async-done | bytes 32800 | tf_op jit(solution)/shard_map/all_to_all | solution.py:67
  382.6 0.1 reshape.129
  382.7 0.1 copy.79
  382.8 0.1 copy.86
  382.9 1.2 gather_fusion.1
  384.1 0.0 copy-done.3
  (14 shorter events, 0.2 us)
Async XLA Ops:
  0.6 2.1 copy-start
  15.2 19.1 %copy-start.4 = (bf16[64,6272]{1,0:T(8,128)(2,1)S(1)}, bf16[64,6272]{1,0:T(8,128)(2,1)}, u32[]{:S(2)}) copy-start(bf16[64,6272]{1,0:T(8,128)(2,1)} %param.8) | copy-start | bytes 2408452
  15.2 166.8 %all-to-all-start = ((bf16[2,128,6272]{2,0,1:T(2,128)(2,1)}), bf16[2,128,6272]{2,0,1:T(2,128)(2,1)}, u32[]{:S(2)}, u32[]{:S(2)}) async-start(bf16[2,128,6272]{2,0,1:T(2,128)(2,1)} %broadcast_select_fusion.1), calls=%async_computation | async-start | bytes 6422528 | tf_op jit(solution)/shard_map/all_to_all | solution.py:34
  201.5 1.7 copy-start.2
  278.7 1.7 copy-start.1
  334.7 49.3 %copy-start.3 = (bf16[2,64,6272]{2,1,0:T(8,128)(2,1)}, bf16[2,64,6272]{2,1,0:T(8,128)(2,1)S(1)}, u32[]{:S(2)}) copy-start(bf16[2,64,6272]{2,1,0:T(8,128)(2,1)S(1)} %convolution_convert_fusion) | copy-start | bytes 4816900
  334.7 34.2 %copy-start.5 = (s32[64,1]{0,1:T(1,128)S(1)}, s32[64,1]{0,1:T(1,128)}, u32[]{:S(2)}) copy-start(s32[64,1]{0,1:T(1,128)} %param.7) | copy-start | bytes 772
  363.0 19.6 %all-to-all-start.1 = ((bf16[64,2,128]{2,1,0:T(2,128)(2,1)}), bf16[64,2,128]{2,1,0:T(2,128)(2,1)S(1)}, u32[]{:S(2)}, u32[]{:S(2)}) async-start(bf16[64,2,128]{2,1,0:T(2,128)(2,1)} %reshape.128), calls=%async_computation.1 | async-start | bytes 65536 | tf_op jit(solution)/shard_map/all_to_all | solution.py:67
